TPU v7x, 32 devices: a whole 2x2x4 slice. The times are simulated.
32 devices in a mesh: row: 8 (over z, x), col: 4 (over y, core).
Axes of the slice: x: 2, y: 2, z: 4, core: 2. Of those that a mesh axis runs over, the one named last changes fastest.
Arguments:
- panel_block: float32 [24576, 512], P('row', 'col'), may hold values from -1 to 1
- trailing: float32 [24576, 2048], P('row', 'col'), may hold values from -6 to 6
Outputs:
- triangle: float32 [512, 512], replicated
- coupling: float32 [512, 2048], P(None, 'col')
- updated: float32 [24576, 2048], P('row', 'col')
All inputs are finite; a program needn't handle non-finite values.
Results may differ from a plain program's by a relative error of at most 0.0003.
Values sent between devices are 32-bit elements; how exact they have to be, the bound alone decides.
A program may use at most 128 MiB of HBM per device.

v0:
```python
import jax
import jax.numpy as jnp
from jax import lax
from jax.sharding import PartitionSpec as P

highest = lax.Precision.HIGHEST


def inner_products(left, right):
    return lax.dot_general(
        left, right, (((0,), (0,)), ((), ())), precision=highest, preferred_element_type=jnp.float32
    )


def matmul(left, right):
    return jnp.dot(left, right, precision=highest, preferred_element_type=jnp.float32)


def leaf_factor(square):
    width = square.shape[0]
    places = jnp.arange(width)
    columns = []
    for index in range(width):
        column_now = square[:, index]
        if index > 0:
            prior = jnp.stack(columns, axis=1)
            column_now = column_now - matmul(prior, prior[index])
        pivot = jnp.sqrt(column_now[index])
        column_now = jnp.where(
            places > index, column_now / pivot, jnp.where(places == index, pivot, 0.0)
        )
        columns.append(column_now)
    return jnp.stack(columns, axis=1)


def leaf_inverse(lower):
    width = lower.shape[0]
    places = jnp.arange(width)
    rows_done = []
    for index in range(width):
        unit_row = (places == index).astype(jnp.float32)
        if index > 0:
            prior = jnp.stack(rows_done, axis=0)
            unit_row = unit_row - matmul(lower[index, :index], prior)
        rows_done.append(unit_row / lower[index, index])
    return jnp.stack(rows_done, axis=0)


def blocked_factor(gram):
    width = gram.shape[0]
    if width <= 16:
        lower = leaf_factor(gram)
        return (lower, leaf_inverse(lower))
    half = width // 2
    upper_lower, upper_inverse = blocked_factor(gram[:half, :half])
    below = matmul(gram[half:, :half], upper_inverse.T)
    schur = gram[half:, half:] - matmul(below, below.T)
    last_lower, last_inverse = blocked_factor(schur)
    corner = -matmul(last_inverse, matmul(below, upper_inverse))
    zero_block = jnp.zeros((half, width - half), jnp.float32)
    full_lower = jnp.block([[upper_lower, zero_block], [below, last_lower]])
    full_inverse = jnp.block([[upper_inverse, zero_block], [corner, last_inverse]])
    return (full_lower, full_inverse)


def on_device(panel_block, trailing):
    gathered = lax.all_gather(panel_block, "col", axis=1, tiled=True)
    local_gram = inner_products(gathered, gathered)
    projected = None
    summed, projected = lax.psum((local_gram, inner_products(gathered, trailing)), "row")
    lower_tri, lower_inv = blocked_factor(summed)
    upper_tri = lower_tri.T
    orthonormal = matmul(gathered, lower_inv.T)
    if projected is None:
        coupling = lax.psum(inner_products(orthonormal, trailing), "row")
    else:
        coupling = matmul(lower_inv, projected)
    updated = trailing - matmul(orthonormal, coupling)
    return (upper_tri, coupling, updated)


def solution(mesh):
    placed = (P("row", "col"), P("row", "col"))
    return jax.shard_map(
        on_device,
        mesh=mesh,
        in_specs=placed,
        out_specs=(P(), P(None, "col"), P("row", "col")),
        check_vma=False,
    )
```

profile of v0, /device:TPU:0, one launch (start us, length us, event | category | flops | bytes accessed | tf_op | source)
XLA Modules:
  0.0 1965.8 jit_solution(4469159194429726247)
XLA Ops:
  7.9 51.5 %all-gather.2.cloned.1.call-done = f32[3072,512]{1,0:T(8,128)} async-done(((f32[3072,128]{1,0:T(8,128)}), f32[3072,512]{1,0:T(8,128)}) %all-gather.2.cloned.1.call-update) | async-done | bytes 6291472 | tf_op jit(solution)/shard_map/all_gather | solution.py:67
  59.5 15.1 fusion.2678
  74.6 11.4 fusion.2709
  86.0 102.4 %all-reduce.49.cloned.1.call-done = (f32[512,512]{1,0:T(8,128)}, f32[512,512]{1,0:T(8,128)}) async-done(((f32[512,512]{1,0:T(8,128)}, f32[512,512]{1,0:T(8,128)}), (f32[512,512]{1,0:T(8,128)}, f32[512,512]{1,0:T(8,128)})) %all-reduce.49.cloned.1.call-update) | async-done | bytes 2097168 | tf_op jit(solution)/shard_map/psum | solution.py:70
  190.4 1.7 slice_reduce_fusion.434
  192.7 1.5 slice_subtract_fusion.31
  1011.3 1.4 fusion.1793
  1012.7 1.5 convolution_subtract_fusion.1
  1297.9 1.3 divide_bitcast_fusion.10
  1822.1 2.3 fusion.2645
  1873.6 1.4 concatenate.1213
  1882.1 1.4 fusion.1791
  1883.5 1.4 fusion.1648
  1884.9 1.4 fusion.1651
  1887.6 1.4 fusion.1654
  1890.3 1.4 fusion.1657
  1893.0 1.4 fusion.1660
  1898.1 1.3 slice.10207
  1905.1 1.4 concatenate.1214
  1906.5 1.4 fusion.1663
  1908.0 1.5 fusion.1011
  1909.5 1.4 fusion.1013
  1910.9 1.5 fusion.1015
  1912.5 1.4 fusion.1017
  1914.0 1.4 fusion.1019
  1915.4 1.4 fusion.1021
  1916.9 1.4 fusion.1023
  1924.5 1.3 copy.15324
  1929.9 1.6 convolution_negate_fusion
  1931.5 3.3 fusion.2644
  1935.0 11.1 fusion.2643
  1946.1 12.7 convolution_subtract_fusion
  (5158 shorter events, 1316.9 us)
Async XLA Ops:
  7.2 52.3 %all-gather.2.cloned.1.call-start = ((), (), s32[]{:S(2)}) async-start(), calls=%async_computation | async-start | bytes 7864320 | tf_op jit(solution)/shard_map/all_gather | solution.py:67
  7.9 180.6 %all-reduce.49.cloned.1.call-start = ((), (), s32[]{:S(2)}) async-start(), calls=%async_computation.1 | async-start | bytes 4194304 | tf_op jit(solution)/shard_map/psum | solution.py:70
  265.9 100.4 %copy-start.110 = (f32[16,1]{1,0:T(8,128)}, f32[16,1]{1,0:T(8,128)S(1)}, u32[]{:S(2)}) copy-start(f32[16,1]{1,0:T(8,128)S(1)} %copy.11774) | copy-start | bytes 196
  267.6 100.4 %copy-start.146 = (f32[16,1]{1,0:T(8,128)}, f32[16,1]{1,0:T(8,128)S(1)}, u32[]{:S(2)}) copy-start(f32[16,1]{1,0:T(8,128)S(1)} %copy.11775) | copy-start | bytes 196
  345.2 173.0 %copy-start.91 = (f32[16,16]{1,0:T(8,128)}, f32[16,16]{1,0:T(8,128)S(1)}, u32[]{:S(2)}) copy-start(f32[16,16]{1,0:T(8,128)S(1)} %fusion.1984) | copy-start | bytes 3076
  368.1 151.7 %copy-start.112 = (f32[16,1]{1,0:T(8,128)}, f32[16,1]{1,0:T(8,128)S(1)}, u32[]{:S(2)}) copy-start(f32[16,1]{1,0:T(8,128)S(1)} %copy.12010) | copy-start | bytes 196
  369.7 194.2 %copy-start.148 = (f32[16,1]{1,0:T(8,128)}, f32[16,1]{1,0:T(8,128)S(1)}, u32[]{:S(2)}) copy-start(f32[16,1]{1,0:T(8,128)S(1)} %copy.12011) | copy-start | bytes 196
  498.7 260.8 %copy-start.5 = (f32[32,32]{1,0:T(8,128)}, f32[32,32]{1,0:T(8,128)S(1)}, u32[]{:S(2)}) copy-start(f32[32,32]{1,0:T(8,128)S(1)} %fusion.1912) | copy-start | bytes 12292
  518.3 259.3 %copy-start.13 = (f32[16,1]{1,0:T(8,128)}, f32[16,1]{1,0:T(8,128)S(1)}, u32[]{:S(2)}) copy-start(f32[16,1]{1,0:T(8,128)S(1)} %copy.12362) | copy-start | bytes 196
  568.9 236.5 %copy-start.14 = (f32[16,1]{1,0:T(8,128)}, f32[16,1]{1,0:T(8,128)S(1)}, u32[]{:S(2)}) copy-start(f32[16,1]{1,0:T(8,128)S(1)} %copy.12480) | copy-start | bytes 196
  572.1 195.5 %copy-start.116 = (f32[16,1]{1,0:T(8,128)}, f32[16,1]{1,0:T(8,128)S(1)}, u32[]{:S(2)}) copy-start(f32[16,1]{1,0:T(8,128)S(1)} %copy.12482) | copy-start | bytes 196
  575.4 254.1 %copy-start.186 = (f32[16,1]{1,0:T(8,128)}, f32[16,1]{1,0:T(8,128)S(1)}, u32[]{:S(2)}) copy-start(f32[16,1]{1,0:T(8,128)S(1)} %copy.12484) | copy-start | bytes 196
  730.3 259.2 %copy-start.189 = (f32[16,1]{1,0:T(8,128)}, f32[16,1]{1,0:T(8,128)S(1)}, u32[]{:S(2)}) copy-start(f32[16,1]{1,0:T(8,128)S(1)} %copy.12838) | copy-start | bytes 196
  774.3 133.7 %copy-start.18 = (f32[16,1]{1,0:T(8,128)}, f32[16,1]{1,0:T(8,128)S(1)}, u32[]{:S(2)}) copy-start(f32[16,1]{1,0:T(8,128)S(1)} %copy.12952) | copy-start | bytes 196
  805.7 208.6 %copy-start.81 = (f32[64,128]{1,0:T(8,128)}, f32[64,128]{1,0:T(8,128)S(1)}, u32[]{:S(2)}) copy-start(f32[64,128]{1,0:T(8,128)S(1)} %concatenate.1133) | copy-start | bytes 98308
  831.0 209.5 %copy-start.157 = (f32[16,1]{1,0:T(8,128)}, f32[16,1]{1,0:T(8,128)S(1)}, u32[]{:S(2)}) copy-start(f32[16,1]{1,0:T(8,128)S(1)} %copy.13073) | copy-start | bytes 196
  876.7 211.2 %copy-start.20 = (f32[16,1]{1,0:T(8,128)}, f32[16,1]{1,0:T(8,128)S(1)}, u32[]{:S(2)}) copy-start(f32[16,1]{1,0:T(8,128)S(1)} %copy.13188) | copy-start | bytes 196
  881.6 129.0 %copy-start.158 = (f32[16,1]{1,0:T(8,128)}, f32[16,1]{1,0:T(8,128)S(1)}, u32[]{:S(2)}) copy-start(f32[16,1]{1,0:T(8,128)S(1)} %copy.13191) | copy-start | bytes 196
  908.0 119.3 %copy-start.86 = (f32[32,64]{1,0:T(8,128)}, f32[32,64]{1,0:T(8,128)S(1)}, u32[]{:S(2)}) copy-start(f32[32,64]{1,0:T(8,128)S(1)} %concatenate.1134) | copy-start | bytes 24580
  927.9 211.4 %copy-start.21 = (f32[16,1]{1,0:T(8,128)}, f32[16,1]{1,0:T(8,128)S(1)}, u32[]{:S(2)}) copy-start(f32[16,1]{1,0:T(8,128)S(1)} %copy.13306) | copy-start | bytes 196
  1010.6 214.2 %copy-start.89 = (f32[16,16]{1,0:T(8,128)}, f32[16,16]{1,0:T(8,128)S(1)}, u32[]{:S(2)}) copy-start(f32[16,16]{1,0:T(8,128)S(1)} %convolution_negate_fusion.23) | copy-start | bytes 3076
  1010.8 206.9 %copy-start.85 = (f32[32,32]{1,0:T(8,128)}, f32[32,32]{1,0:T(8,128)S(1)}, u32[]{:S(2)}) copy-start(f32[32,32]{1,0:T(8,128)S(1)} %convolution_negate_fusion.11) | copy-start | bytes 12292
  1011.1 206.7 %copy-start.82 = (f32[64,64]{1,0:T(8,128)}, f32[64,64]{1,0:T(8,128)S(1)}, u32[]{:S(2)}) copy-start(f32[64,64]{1,0:T(8,128)S(1)} %convolution_negate_fusion.5) | copy-start | bytes 49156
  1033.9 184.1 %copy-start.23 = (f32[16,1]{1,0:T(8,128)}, f32[16,1]{1,0:T(8,128)S(1)}, u32[]{:S(2)}) copy-start(f32[16,1]{1,0:T(8,128)S(1)} %copy.13544) | copy-start | bytes 196
  1084.7 133.3 %copy-start.24 = (f32[16,1]{1,0:T(8,128)}, f32[16,1]{1,0:T(8,128)S(1)}, u32[]{:S(2)}) copy-start(f32[16,1]{1,0:T(8,128)S(1)} %copy.13662) | copy-start | bytes 196
  1167.0 103.5 %copy-start.99 = (f32[16,16]{1,0:T(8,128)}, f32[16,16]{1,0:T(8,128)S(1)}, u32[]{:S(2)}) copy-start(f32[16,16]{1,0:T(8,128)S(1)} %fusion.1968) | copy-start | bytes 3076
  1319.5 102.8 %copy-start.6 = (f32[32,32]{1,0:T(8,128)}, f32[32,32]{1,0:T(8,128)S(1)}, u32[]{:S(2)}) copy-start(f32[32,32]{1,0:T(8,128)S(1)} %fusion.1904) | copy-start | bytes 12292
  1390.7 133.2 %copy-start.30 = (f32[16,1]{1,0:T(8,128)}, f32[16,1]{1,0:T(8,128)S(1)}, u32[]{:S(2)}) copy-start(f32[16,1]{1,0:T(8,128)S(1)} %copy.14370) | copy-start | bytes 196
  1524.1 217.5 %copy-start.4 = (f32[32,32]{1,0:T(8,128)}, f32[32,32]{1,0:T(8,128)S(1)}, u32[]{:S(2)}) copy-start(f32[32,32]{1,0:T(8,128)S(1)} %fusion.1902) | copy-start | bytes 12292
  1574.7 153.7 %copy-start.103 = (f32[16,16]{1,0:T(8,128)}, f32[16,16]{1,0:T(8,128)S(1)}, u32[]{:S(2)}) copy-start(f32[16,16]{1,0:T(8,128)S(1)} %fusion.1960) | copy-start | bytes 3076
  1594.4 134.9 %copy-start.34 = (f32[16,1]{1,0:T(8,128)}, f32[16,1]{1,0:T(8,128)S(1)}, u32[]{:S(2)}) copy-start(f32[16,1]{1,0:T(8,128)S(1)} %copy.14842) | copy-start | bytes 196
  1699.5 98.4 %copy-start.75 = (f32[16,1]{1,0:T(8,128)}, f32[16,1]{1,0:T(8,128)S(1)}, u32[]{:S(2)}) copy-start(f32[16,1]{1,0:T(8,128)S(1)} %copy.15079) | copy-start | bytes 196
  (199 other events, 6906.5 us)
Sparse Core Ops, SparseCore 0:
  9.5 49.9 all-gather.1
  86.2 102.2 all-reduce.48
where the time goes:
time: 1980 us; the launch traced here: 1970 us
  local copies, waits for them, and re-layouts  782 us (39%)
  matrix products  501 us (25%)
  between operations  405 us (20%)
  waiting for transfers between devices  155 us (8%)
  other arithmetic  124 us (6%)
    dot_general x1023, matrix products, matmul(): jnp.dot(left, right, precision=highest, preferred_element_type=jnp.float32)  474 us
    slice x512, local copies, waits for them, and re-layouts, leaf_factor(): pivot = jnp.sqrt(column_now[index])  303 us
    slice x482, local copies, waits for them, and re-layouts, leaf_inverse(): rows_done.append(unit_row / lower[index, index])  297 us
    psum x1, waiting for transfers between devices, on_device(): lax.psum((local_gram, inner_products(gathered, trailing)), 'row')  102 us
    another operation x480, local copies, waits for them, and re-layouts, leaf_factor(): return jnp.stack(columns, axis=1)  60.6 us
    all_gather x1, waiting for transfers between devices, on_device(): gathered = lax.all_gather(panel_block, 'col', axis=1, tiled=True)  51.5 us
    another operation x32, other arithmetic, leaf_inverse(): return jnp.stack(rows_done, axis=0)  40.5 us

commit v1 on v0

v1 whole, which is shorter than its diff:
```python
import jax
import jax.numpy as jnp
from jax import lax
from jax.experimental import pallas as pl
from jax.experimental.pallas import tpu as pltpu
from jax.sharding import PartitionSpec as P

LANES = 128
SUB = 8
highest = lax.Precision.HIGHEST
high = lax.Precision.HIGH


def inner_products(left, right, precision=high):
    return lax.dot_general(
        left, right, (((0,), (0,)), ((), ())), precision=precision, preferred_element_type=jnp.float32
    )


def matmul(left, right, precision=high):
    return jnp.dot(left, right, precision=precision, preferred_element_type=jnp.float32)


def split3(x):
    top = x.astype(jnp.bfloat16).astype(jnp.float32)
    rest = x - top
    mid = rest.astype(jnp.bfloat16).astype(jnp.float32)
    return top, mid, rest - mid


def rank_update(left, right):
    lt, lm, ll = split3(left)
    rt, rm, rl = split3(right)
    a = jnp.concatenate([lt, lt, lm, lt, ll, lm], axis=0).astype(jnp.bfloat16)
    b = jnp.concatenate([rt, rm, rt, rl, rt, rm], axis=0).astype(jnp.bfloat16)
    return lax.dot_general(a, b, (((0,), (0,)), ((), ())), preferred_element_type=jnp.float32)


def factor_diagonal(square):
    lane = lax.broadcasted_iota(jnp.int32, (SUB, LANES), 1)
    sub = lax.broadcasted_iota(jnp.int32, (SUB, LANES), 0)
    full = (SUB, LANES)
    work = square
    upper_rows, inverse_rows = [], []
    for first in range(0, LANES, SUB):
        rows = work[:SUB]
        b = [jnp.broadcast_to(rows[t : t + 1, :], full) for t in range(SUB)]
        d = [
            [None if s < t else jnp.broadcast_to(b[t][:, first + s : first + s + 1], full) for s in range(SUB)]
            for t in range(SUB)
        ]
        inside = (lane >= first) & (lane < first + SUB)
        unit = [jnp.where(inside, jnp.where(lane == first + t, 1.0, 0.0), b[t]) for t in range(SUB)]
        tri = jnp.zeros(full, jnp.float32)
        out = jnp.zeros(full, jnp.float32)
        for t in range(SUB):
            inv = 1.0 / jnp.sqrt(d[t][t])
            for s in range(t, SUB):
                d[t][s] = d[t][s] * inv
            x = unit[t] * inv
            for s in range(t + 1, SUB):
                for q in range(s, SUB):
                    d[s][q] = d[s][q] - d[t][s] * d[t][q]
                unit[s] = unit[s] - d[t][s] * x
            line = x
            for s in range(SUB):
                line = jnp.where(lane == first + s, d[t][s] if s >= t else 0.0, line)
            tri = jnp.where(sub == t, line, tri)
            out = jnp.where(sub == t, x, out)
        upper_rows.append(jnp.where(lane >= first, tri, 0.0))
        inverse_rows.append(jnp.where(lane < first + SUB, out, 0.0))
        if first + SUB < LANES:
            beyond = jnp.where(lane >= first + SUB, out, 0.0)
            left = work[SUB:]
            place = lax.broadcasted_iota(jnp.int32, left.shape, 1)
            left = jnp.where((place >= first) & (place < first + SUB), 0.0, left)
            work = left - rank_update(beyond, out)[first + SUB :]
    return jnp.concatenate(upper_rows, axis=0), jnp.concatenate(inverse_rows, axis=0)


def factor_kernel(gram_ref, upper_ref, inverse_ref, work):
    width = gram_ref.shape[0]
    work[...] = gram_ref[...]
    upper_ref[...] = jnp.zeros_like(upper_ref)
    inverse_ref[...] = jnp.zeros_like(inverse_ref)
    lanes_all = lax.broadcasted_iota(jnp.int32, (LANES, width), 1)

    @pl.loop(0, width // LANES)
    def _(k):
        at = pl.multiple_of(k * LANES, LANES)
        here = pl.ds(at, LANES)
        upper, inverse = factor_diagonal(work[here, here])
        rows = matmul(inverse, work[here, :], highest)
        upper_ref[here, :] = jnp.where(lanes_all >= at + LANES, rows, 0.0)
        upper_ref[here, here] = upper
        inverse_ref[here, :] = jnp.where(lanes_all < at, rows, 0.0)
        inverse_ref[here, here] = inverse
        work[here, :] = rows
        work[here, here] = inverse
        done = work[here, :]
        right = upper_ref[here, :]
        for i in range(1, width // LANES):
            @pl.when(i > k)
            def _():
                block = slice(i * LANES, (i + 1) * LANES)
                below = inner_products(right[:, block], done, highest)
                old = jnp.where((lanes_all >= at) & (lanes_all < at + LANES), 0.0, work[block, :])
                work[block, :] = old - below


def factor(gram):
    width = gram.shape[0]
    spec = pl.BlockSpec(memory_space=pltpu.VMEM)
    shape = jax.ShapeDtypeStruct((width, width), jnp.float32)
    return pl.pallas_call(
        factor_kernel,
        out_shape=(shape, shape),
        in_specs=[spec],
        out_specs=(spec, spec),
        scratch_shapes=[pltpu.VMEM((width, width), jnp.float32)],
        cost_estimate=pl.CostEstimate(
            flops=4 * width**3, bytes_accessed=12 * width * width, transcendentals=100000
        ),
        name="factor",
    )(gram)


def on_device(panel_block, trailing):
    gathered = lax.all_gather(panel_block, "col", axis=1, tiled=True)
    gram_part = lax.psum(inner_products(gathered, panel_block), "row")
    gram = lax.all_gather(gram_part, "col", axis=1, tiled=True)
    share = inner_products(gathered, trailing)
    gram, share = lax.optimization_barrier((gram, share))
    projected = lax.psum(share, "row")
    upper, inverse = factor(gram)
    coupling = matmul(inverse, projected)
    weights = inner_products(inverse, coupling)
    updated = trailing - matmul(gathered, weights)
    return (upper, coupling, updated)


def solution(mesh):
    placed = (P("row", "col"), P("row", "col"))
    return jax.shard_map(
        on_device,
        mesh=mesh,
        in_specs=placed,
        out_specs=(P(), P(None, "col"), P("row", "col")),
        check_vma=False,
    )
```

time: 1980 us -> 274 us (0.14)
  local copies, waits for them, and re-layouts: 782 us -> 13.1 us
  matrix products: 501 us -> 44.4 us
  between operations: 405 us -> 13.8 us
  other arithmetic: 124 us -> 0 us
  Pallas kernels: 0 us -> 33.4 us
    slice x1120 -> x0, local copies, waits for them, and re-layouts: 635 us -> none  [the longest x512 303 us: leaf_factor(): pivot = jnp.sqrt(column_now[index])]
    dot_general x1025 -> x5, matrix products: 501 us -> 44.4 us  [the longest x3 26.4 us: inner_products(): lax.dot_general(left, right, (((0,), (0,)), ((), ())), precision=precisio...]
    another operation x1217 -> x0, local copies, waits for them, and re-layouts: 108 us -> none  [the longest x480 60.6 us: leaf_factor(): return jnp.stack(columns, axis=1)]
    another operation x608 -> x0, other arithmetic: 62.1 us -> none  [the longest x32 40.5 us: leaf_inverse(): return jnp.stack(rows_done, axis=0)]
    pallas_call x0 -> x1, Pallas kernels: none -> 33.4 us  [factor(): pl.pallas_call(factor_kernel, out_shape=(shape, shape), in_specs=[spec],...]
    concatenate x47 -> x0, local copies, waits for them, and re-layouts: 31.3 us -> none  [the longest x32 28.8 us: blocked_factor(): full_lower = jnp.block([[upper_lower, zero_block], [below, last_lower]])]
    sub x32 -> x0, other arithmetic: 23.4 us -> none  [leaf_factor(): column_now = column_now - matmul(prior, prior[index])]
    psum x1 -> x2, waiting for transfers between devices: 102 us -> 114 us  [the longest x1 71.2 us: on_device(): gram_part = lax.psum(inner_products(gathered, panel_block), 'row')]
where the time goes in v1:
time: 274 us
  waiting for transfers between devices  169 us (62%)
  matrix products  44.4 us (16%)
  Pallas kernels  33.4 us (12%)
  between operations  13.8 us (5%)
  local copies, waits for them, and re-layouts  13.1 us (5%)
    psum x1, waiting for transfers between devices, on_device(): gram_part = lax.psum(inner_products(gathered, panel_block), 'row')  71.2 us
    all_gather x1, waiting for transfers between devices, on_device(): gathered = lax.all_gather(panel_block, 'col', axis=1, tiled=True)  51.5 us
    psum x1, waiting for transfers between devices, on_device(): projected = lax.psum(share, 'row')  42.5 us
    pallas_call x1, Pallas kernels, factor(): pl.pallas_call(factor_kernel, out_shape=(shape, shape), in_specs=[spec],...  33.4 us
    dot_general x3, matrix products, inner_products(): lax.dot_general(left, right, (((0,), (0,)), ((), ())), precision=precisio...  26.4 us
    dot_general x2, matrix products, matmul(): jnp.dot(left, right, precision=precision, preferred_element_type=jnp.floa...  18 us
    unnamed x6, local copies, waits for them, and re-layouts  13.1 us
  transfers between devices with their start and end apart: 4, of which 4 were waited for; matrix products, arithmetic and copies ran while one was open for 8% of the time, Pallas kernels for 12%

profile of v1, /device:TPU:0, one launch (start us, length us, event | category | flops | bytes accessed | tf_op | source)
XLA Modules:
  0.0 273.5 jit_solution(15337466557778825178)
XLA Ops:
  7.2 0.0 all-gather.3.cloned.1.call-start
  7.2 0.7 all-gather.3.cloned.1.call-update
  7.9 0.0 all-reduce.3.cloned.1.call-start
  7.9 51.5 %all-gather.3.cloned.1.call-done = f32[3072,512]{1,0:T(8,128)} async-done(((f32[3072,128]{1,0:T(8,128)}), f32[3072,512]{1,0:T(8,128)}) %all-gather.3.cloned.1.call-update) | async-done | bytes 6291472 | tf_op jit(solution)/shard_map/all_gather | solution.py:129
  59.5 9.0 %fusion = f32[512,128]{1,0:T(8,128)} fusion(f32[3072,512]{1,0:T(8,128)} %all-gather.3.cloned.1.call-done, f32[3072,128]{1,0:T(8,128)} %param.2), kind=kOutput, calls=%fused_computation.1 | convolution fusion | flops 1207959552 | bytes 8126464 | tf_op jit(solution)/shard_map/dot_general | solution.py:15
  68.4 0.0 all-reduce.3.cloned.1.call-update
  68.5 0.0 all-gather.5.cloned.1.call-start
  68.5 71.2 %all-reduce.3.cloned.1.call-done = f32[512,128]{1,0:T(8,128)} async-done(((f32[512,128]{1,0:T(8,128)}), f32[512,128]{1,0:T(8,128)}) %all-reduce.3.cloned.1.call-update) | async-done | bytes 262160 | tf_op jit(solution)/shard_map/psum | solution.py:130
  139.7 0.0 all-gather.5.cloned.1.call-update
  139.7 0.2 all-reduce.5.cloned.1.call-start
  139.9 14.8 %fusion.1 = f32[512,512]{1,0:T(8,128)} fusion(f32[3072,512]{1,0:T(8,128)} %all-gather.3.cloned.1.call-done, f32[3072,512]{1,0:T(8,128)} %param.3), kind=kOutput, calls=%fused_computation.2 | convolution fusion | flops 4831838208 | bytes 13631488 | tf_op jit(solution)/shard_map/dot_general | solution.py:15
  154.7 2.6 all-gather.5.cloned.1.call-done.gram_ref
  157.3 0.0 all-reduce.5.cloned.1.call-update
  157.3 6.6 %copy.5 = f32[3072,512]{0,1:T(8,128)} copy(f32[3072,512]{1,0:T(8,128)} %param.3) | data formatting | bytes 12582912 | tf_op args[1]
  163.9 33.4 %factor.1 = (f32[512,512]{1,0:T(8,128)}, f32[512,512]{1,0:T(8,128)}) custom-call(f32[512,512]{1,0:T(8,128)} %all-gather.5.cloned.1.call-done.gram_ref), custom_call_target="tpu_custom_call" | custom-call | flops 536870912 | bytes 3145728 | tf_op jit(solution)/shard_map/factor/pallas_call | solution.py:115
  197.2 42.5 %all-reduce.5.cloned.1.call-done = f32[512,512]{1,0:T(8,128)} async-done(((f32[512,512]{1,0:T(8,128)}), f32[512,512]{1,0:T(8,128)}) %all-reduce.5.cloned.1.call-update) | async-done | bytes 1048592 | tf_op jit(solution)/shard_map/psum | solution.py:134
  239.8 0.0 copy-start
  239.8 2.7 fusion.2
  242.5 0.0 copy-start.1
  242.5 2.6 fusion.3
  245.1 0.0 copy-done
  245.1 15.3 %bitcast_subtract_fusion = f32[3072,512]{0,1:T(8,128)} fusion(f32[3072,512]{0,1:T(8,128)S(1)} %copy-done, f32[512,512]{1,0:T(8,128)S(1)} %fusion.3, f32[3072,512]{1,0:T(8,128)} %all-gather.3.cloned.1.call-done), kind=kOutput, calls=%fused_computation | convolution fusion | flops 4833411072 | bytes 19922944 | tf_op jit(solution)/shard_map/dot_general | solution.py:21
  260.4 0.0 copy-done.1
  260.5 6.6 %copy.6 = f32[3072,512]{1,0:T(8,128)} copy(f32[3072,512]{0,1:T(8,128)} %bitcast_subtract_fusion) | data formatting | bytes 12582912
Async XLA Ops:
  7.2 52.3 %all-gather.3.cloned.1.call-start = ((), (), s32[]{:S(2)}) async-start(), calls=%async_computation | async-start | bytes 7864320 | tf_op jit(solution)/shard_map/all_gather | solution.py:129
  7.9 131.8 %all-reduce.3.cloned.1.call-start = ((), (), s32[]{:S(2)}) async-start(), calls=%async_computation.1 | async-start | bytes 524288 | tf_op jit(solution)/shard_map/psum | solution.py:130
  68.5 88.8 %all-gather.5.cloned.1.call-start = ((), (), s32[]{:S(2)}) async-start(), calls=%async_computation.2 | async-start | bytes 1310720 | tf_op jit(solution)/shard_map/all_gather | solution.py:131
  139.7 100.1 %all-reduce.5.cloned.1.call-start = ((), (), s32[]{:S(2)}) async-start(), calls=%async_computation.3 | async-start | bytes 2097152 | tf_op jit(solution)/shard_map/psum | solution.py:134
  239.8 5.3 %copy-start = (f32[3072,512]{0,1:T(8,128)S(1)}, f32[3072,512]{0,1:T(8,128)}, u32[]{:S(2)}) copy-start(f32[3072,512]{0,1:T(8,128)} %copy.5) | copy-start | bytes 18874372
  242.5 18.0 %copy-start.1 = (f32[512,512]{1,0:T(8,128)}, f32[512,512]{1,0:T(8,128)S(1)}, u32[]{:S(2)}) copy-start(f32[512,512]{1,0:T(8,128)S(1)} %fusion.2) | copy-start | bytes 3145732
Sparse Core Ops, SparseCore 0:
  9.5 49.9 all-gather.2
  68.6 71.0 all-reduce.2
  141.2 16.0 all-gather.4
  161.2 78.4 all-reduce.4

commit v2 on v1

--- a/solution.py
+++ b/solution.py
@@ -1,3 +1,5 @@
+import functools
+
 import jax
 import jax.numpy as jnp
 from jax import lax
@@ -125,24 +127,177 @@
     )(gram)
 
 
-def on_device(panel_block, trailing):
+def gram_kernel(nr, nc, part_ref, out_ref, heard, total, blocks, send, recv, give, take, pass_on, get):
+    my_row = lax.axis_index("row")
+    my_col = lax.axis_index("col")
+    size = part_ref.shape[0] // nr
+    wide = part_ref.shape[1]
+    mesh_id = pl.DeviceIdType.MESH
+
+    def rows_of(row):
+        return pl.ds(pl.multiple_of(row * size, size), size)
+
+    def row_peer(k):
+        return lax.rem(my_row + k, nr)
+
+    def col_peer(j):
+        return lax.rem(my_col + j, nc)
+
+    barrier = pltpu.get_barrier_semaphore()
+    for k in range(1, nr):
+        pl.semaphore_signal(barrier, inc=1, device_id=(row_peer(k), my_col), device_id_type=mesh_id)
+    for j in range(1, nc):
+        pl.semaphore_signal(barrier, inc=1, device_id=(my_row, col_peer(j)), device_id_type=mesh_id)
+    pl.semaphore_wait(barrier, nr + nc - 2)
+
+    first = [
+        pltpu.make_async_remote_copy(
+            src_ref=part_ref.at[rows_of(row_peer(k))],
+            dst_ref=heard.at[k],
+            send_sem=send.at[k],
+            recv_sem=recv.at[k],
+            device_id=(row_peer(k), my_col),
+            device_id_type=mesh_id,
+        )
+        for k in range(1, nr)
+    ]
+    for copy in first:
+        copy.start()
+    value = part_ref[rows_of(my_row), :]
+    for k, copy in enumerate(first, 1):
+        copy.wait_recv()
+        value = value + heard[k]
+    total[...] = value
+
+    def spread(k, j, block):
+        return pltpu.make_async_remote_copy(
+            src_ref=block,
+            dst_ref=blocks.at[my_col, rows_of(lax.rem(my_row - k + nr, nr))],
+            send_sem=pass_on.at[k, j],
+            recv_sem=get.at[k, j],
+            device_id=(my_row, col_peer(j)),
+            device_id_type=mesh_id,
+        )
+
+    second = [
+        pltpu.make_async_remote_copy(
+            src_ref=total,
+            dst_ref=blocks.at[my_col, rows_of(my_row)],
+            send_sem=give.at[k],
+            recv_sem=take.at[k],
+            device_id=(row_peer(k), my_col),
+            device_id_type=mesh_id,
+        )
+        for k in range(1, nr)
+    ]
+    for copy in second:
+        copy.start()
+    third = [spread(0, j, total) for j in range(1, nc)]
+    for copy in third:
+        copy.start()
+    blocks[my_col, rows_of(my_row), :] = value
+    for k, copy in enumerate(second, 1):
+        copy.wait_recv()
+        block = blocks.at[my_col, rows_of(lax.rem(my_row - k + nr, nr))]
+        for j in range(1, nc):
+            hop = spread(k, j, block)
+            hop.start()
+            third.append(hop)
+    for copy in third:
+        copy.wait_recv()
+    for c in range(nc):
+        out_ref[:, c * wide : (c + 1) * wide] = blocks[c]
+    for copy in first + second + third:
+        copy.wait_send()
+
+
+def sum_gram(part, nr, nc):
+    width, wide = part.shape
+    spec = pl.BlockSpec(memory_space=pltpu.VMEM)
+    dma = pltpu.SemaphoreType.DMA
+    return pl.pallas_call(
+        functools.partial(gram_kernel, nr, nc),
+        out_shape=jax.ShapeDtypeStruct((width, wide * nc), jnp.float32),
+        in_specs=[spec],
+        out_specs=spec,
+        scratch_shapes=[
+            pltpu.VMEM((nr, width // nr, wide), jnp.float32),
+            pltpu.VMEM((width // nr, wide), jnp.float32),
+            pltpu.VMEM((nc, width, wide), jnp.float32),
+            dma((nr,)),
+            dma((nr,)),
+            dma((nr,)),
+            dma((nr,)),
+            dma((nr, nc)),
+            dma((nr, nc)),
+        ],
+        compiler_params=pltpu.CompilerParams(collective_id=0, has_side_effects=True),
+        cost_estimate=pl.CostEstimate(
+            flops=100000, bytes_accessed=20000000, transcendentals=0
+        ),
+        name="sum_gram",
+    )(part)
+
+
+def split2(x):
+    top = x.astype(jnp.bfloat16)
+    return top, (x - top.astype(jnp.float32)).astype(jnp.bfloat16)
+
+
+def update_kernel(panel_ref, weights_ref, trailing_ref, out_ref, top, low):
+    @pl.when(pl.program_id(0) == 0)
+    def _():
+        top[...], low[...] = split2(weights_ref[...])
+
+    pt, pm = split2(panel_ref[...])
+
+    def product(left, right):
+        return jnp.dot(left, right[...], preferred_element_type=jnp.float32)
+
+    out_ref[...] = trailing_ref[...] - (product(pt, top) + (product(pt, low) + product(pm, top)))
+
+
+def update(panel, weights, trailing):
+    rows, width = panel.shape
+    columns = trailing.shape[1]
+    tile = next((t for t in (384, 256, 128, 64, 8) if rows % t == 0), rows)
+    return pl.pallas_call(
+        update_kernel,
+        grid=(rows // tile,),
+        out_shape=jax.ShapeDtypeStruct(trailing.shape, jnp.float32),
+        in_specs=[
+            pl.BlockSpec((tile, width), lambda i: (i, 0)),
+            pl.BlockSpec((width, columns), lambda i: (0, 0)),
+            pl.BlockSpec((tile, columns), lambda i: (i, 0)),
+        ],
+        out_specs=pl.BlockSpec((tile, columns), lambda i: (i, 0)),
+        scratch_shapes=[pltpu.VMEM((width, columns), jnp.bfloat16)] * 2,
+        cost_estimate=pl.CostEstimate(
+            flops=6 * rows * width * columns,
+            bytes_accessed=4 * (rows * width + 2 * rows * columns),
+            transcendentals=0,
+        ),
+        name="update",
+    )(panel, weights, trailing)
+
+
+def on_device(nr, nc, panel_block, trailing):
     gathered = lax.all_gather(panel_block, "col", axis=1, tiled=True)
-    gram_part = lax.psum(inner_products(gathered, panel_block), "row")
-    gram = lax.all_gather(gram_part, "col", axis=1, tiled=True)
     share = inner_products(gathered, trailing)
-    gram, share = lax.optimization_barrier((gram, share))
     projected = lax.psum(share, "row")
+    gathered, share = lax.optimization_barrier((gathered, share))
+    gram = sum_gram(inner_products(gathered, panel_block), nr, nc)
     upper, inverse = factor(gram)
     coupling = matmul(inverse, projected)
     weights = inner_products(inverse, coupling)
-    updated = trailing - matmul(gathered, weights)
+    updated = update(gathered, weights, trailing)
     return (upper, coupling, updated)
 
 
 def solution(mesh):
     placed = (P("row", "col"), P("row", "col"))
     return jax.shard_map(
-        on_device,
+        functools.partial(on_device, mesh.shape["row"], mesh.shape["col"]),
         mesh=mesh,
         in_specs=placed,
         out_specs=(P(), P(None, "col"), P("row", "col")),

time: 274 us -> 186 us (0.68)
  waiting for transfers between devices: 169 us -> 62.1 us
  Pallas kernels: 33.4 us -> 79.9 us
  matrix products: 44.4 us -> 29.5 us
  local copies, waits for them, and re-layouts: 13.1 us -> 0.01 us
    psum x1 -> x0, waiting for transfers between devices: 71.2 us -> none  [on_device(): gram_part = lax.psum(inner_products(gathered, panel_block), 'row')]
    pallas_call x0 -> x2, Pallas kernels: none -> 46.5 us  [the longest x1 34.4 us: sum_gram(): pl.pallas_call(functools.partial(gram_kernel, nr, nc), out_shape=jax.Shap...]
    psum x1, waiting for transfers between devices: 42.5 us -> 9.92 us  [on_device(): projected = lax.psum(share, 'row')]
    dot_general x2 -> x1, matrix products: 18 us -> 2.54 us  [matmul(): jnp.dot(left, right, precision=precision, preferred_element_type=jnp.floa...]
    unnamed x6 -> x4, local copies, waits for them, and re-layouts: 13.1 us -> 0.01 us
  transfers between devices with their start and end apart: 4 -> 2, of which waited for: 4 -> 2; matrix products, arithmetic and copies ran while one was open for 8% -> 5% of each run, Pallas kernels for 12% -> 37%
where the time goes in v2:
time: 186 us
  Pallas kernels  79.9 us (43%)
  waiting for transfers between devices  62.1 us (33%)
  matrix products  29.5 us (16%)
  between operations  14.1 us (8%)
    all_gather x1, waiting for transfers between devices, on_device(): gathered = lax.all_gather(panel_block, 'col', axis=1, tiled=True)  51.5 us
    pallas_call x1, Pallas kernels, sum_gram(): pl.pallas_call(functools.partial(gram_kernel, nr, nc), out_shape=jax.Shap...  34.4 us
    pallas_call x1, Pallas kernels, factor(): pl.pallas_call(factor_kernel, out_shape=(shape, shape), in_specs=[spec],...  33.4 us
    dot_general x3, matrix products, inner_products(): lax.dot_general(left, right, (((0,), (0,)), ((), ())), precision=precisio...  26.9 us
    pallas_call x1, Pallas kernels, update(): pl.pallas_call(update_kernel, grid=(rows // tile,), out_shape=jax.ShapeDt...  12 us
    psum x1, waiting for transfers between devices, on_device(): projected = lax.psum(share, 'row')  9.92 us
  transfers between devices with their start and end apart: 2, of which 2 were waited for; matrix products, arithmetic and copies ran while one was open for 5% of the time, Pallas kernels for 37%

profile of v2, /device:TPU:0, one launch (start us, length us, event | category | flops | bytes accessed | tf_op | source)
XLA Modules:
  0.0 185.7 jit_solution(5168939657641004356)
XLA Ops:
  7.2 0.0 all-gather.2.cloned.1.call-start
  7.2 0.7 all-gather.2.cloned.1.call-update
  7.9 0.0 copy-start
  7.9 0.0 all-reduce.2.cloned.1.call-start
  8.0 51.5 %all-gather.2.cloned.1.call-done.panel_ref = f32[3072,512]{1,0:T(8,128)} async-done(((f32[3072,128]{1,0:T(8,128)}), f32[3072,512]{1,0:T(8,128)}) %all-gather.2.cloned.1.call-update) | async-done | bytes 6291472 | tf_op jit(solution)/shard_map/all_gather | solution.py:285
  59.5 14.8 %fusion = f32[512,512]{1,0:T(8,128)} fusion(f32[3072,512]{1,0:T(8,128)} %all-gather.2.cloned.1.call-done.panel_ref, f32[3072,512]{1,0:T(8,128)} %trailing_ref.1), kind=kOutput, calls=%fused_computation | convolution fusion | flops 4831838208 | bytes 13631488 | tf_op jit(solution)/shard_map/dot_general | solution.py:17
  74.2 0.0 all-reduce.2.cloned.1.call-update
  74.3 0.0 copy-done
  74.3 8.5 %fusion.1.part_ref = f32[512,128]{1,0:T(8,128)} fusion(f32[3072,512]{1,0:T(8,128)} %all-gather.2.cloned.1.call-done.panel_ref, f32[3072,128]{1,0:T(8,128)S(1)} %copy-done), kind=kOutput, calls=%fused_computation.1 | convolution fusion | flops 1207959552 | bytes 8126464 | tf_op jit(solution)/shard_map/dot_general | solution.py:17
  82.8 34.4 %sum_gram.1.gram_ref = f32[512,512]{1,0:T(8,128)} custom-call(f32[512,128]{1,0:T(8,128)} %fusion.1.part_ref), custom_call_target="tpu_custom_call" | custom-call | flops 100000 | bytes 20000000 | tf_op jit(solution)/shard_map/sum_gram/pallas_call | solution.py:218
  117.3 33.4 %factor.1 = (f32[512,512]{1,0:T(8,128)}, f32[512,512]{1,0:T(8,128)}) custom-call(f32[512,512]{1,0:T(8,128)} %sum_gram.1.gram_ref), custom_call_target="tpu_custom_call" | custom-call | flops 536870912 | bytes 3145728 | tf_op jit(solution)/shard_map/factor/pallas_call | solution.py:117
  150.7 9.9 %all-reduce.2.cloned.1.call-done = f32[512,512]{1,0:T(8,128)} async-done(((f32[512,512]{1,0:T(8,128)}), f32[512,512]{1,0:T(8,128)}) %all-reduce.2.cloned.1.call-update) | async-done | bytes 1048592 | tf_op jit(solution)/shard_map/psum | solution.py:287
  160.6 2.5 %fusion.2 = f32[512,512]{1,0:T(8,128)S(1)} fusion(f32[512,512]{1,0:T(8,128)} %get-tuple-element.8, f32[512,512]{1,0:T(8,128)} %all-reduce.2.cloned.1.call-done), kind=kOutput, calls=%fused_computation.2 | convolution fusion | flops 805306368 | bytes 3145728 | tf_op jit(solution)/shard_map/dot_general | solution.py:23
  163.2 0.0 copy-start.1
  163.2 3.6 %fusion.3.weights_ref = f32[512,512]{1,0:T(8,128)} fusion(f32[512,512]{1,0:T(8,128)} %get-tuple-element.8, f32[512,512]{1,0:T(8,128)S(1)} %fusion.2), kind=kOutput, calls=%fused_computation.3 | convolution fusion | flops 805306368 | bytes 3145728 | tf_op jit(solution)/shard_map/dot_general | solution.py:17
  166.8 12.0 %update.1 = f32[3072,512]{1,0:T(8,128)} custom-call(f32[3072,512]{1,0:T(8,128)} %all-gather.2.cloned.1.call-done.panel_ref, f32[512,512]{1,0:T(8,128)} %fusion.3.weights_ref, f32[3072,512]{1,0:T(8,128)} %trailing_ref.1), custom_call_target="tpu_custom_call" | custom-call | flops 4831838208 | bytes 18874368 | tf_op jit(solution)/shard_map/update/pallas_call | solution.py:264
  178.8 0.0 copy-done.1
Async XLA Ops:
  7.2 52.3 %all-gather.2.cloned.1.call-start = ((), (), s32[]{:S(2)}) async-start(), calls=%async_computation | async-start | bytes 7864320 | tf_op jit(solution)/shard_map/all_gather | solution.py:285
  7.9 66.4 %copy-start = (f32[3072,128]{1,0:T(8,128)S(1)}, f32[3072,128]{1,0:T(8,128)}, u32[]{:S(2)}) copy-start(f32[3072,128]{1,0:T(8,128)} %param.2) | copy-start | bytes 4718596
  7.9 152.7 %all-reduce.2.cloned.1.call-start = ((), (), s32[]{:S(2)}) async-start(), calls=%async_computation.1 | async-start | bytes 2097152 | tf_op jit(solution)/shard_map/psum | solution.py:287
  163.2 15.7 %copy-start.1 = (f32[512,512]{1,0:T(8,128)}, f32[512,512]{1,0:T(8,128)S(1)}, u32[]{:S(2)}) copy-start(f32[512,512]{1,0:T(8,128)S(1)} %fusion.2) | copy-start | bytes 3145732
Sparse Core Ops, SparseCore 0:
  9.5 49.9 all-gather.1
  74.4 86.1 all-reduce.1

commit v3 on v2

--- a/solution.py
+++ b/solution.py
@@ -281,8 +281,82 @@
     )(panel, weights, trailing)
 
 
+def gather_kernel(nc, pieces, block_ref, out_ref, send, recv, pass_on, get, near):
+    my_row = lax.axis_index("row")
+    my_col = lax.axis_index("col")
+    rows, wide = block_ref.shape
+    size = rows // pieces
+    mesh_id = pl.DeviceIdType.MESH
+    core = lax.rem(my_col, 2)
+    partner = my_col + 1 - 2 * core
+
+    def across(j):
+        return lax.rem(my_col + 2 * j, nc)
+
+    def columns(col):
+        return pl.ds(pl.multiple_of(col * wide, wide), wide)
+
+    def remote(src, dst, send_sem, recv_sem, col):
+        return pltpu.make_async_remote_copy(
+            src_ref=src, dst_ref=dst, send_sem=send_sem, recv_sem=recv_sem,
+            device_id=(my_row, col), device_id_type=mesh_id,
+        )
+
+    barrier = pltpu.get_barrier_semaphore()
+    pl.semaphore_signal(barrier, inc=1, device_id=(my_row, partner), device_id_type=mesh_id)
+    for j in range(1, nc // 2):
+        pl.semaphore_signal(barrier, inc=1, device_id=(my_row, across(j)), device_id_type=mesh_id)
+    pl.semaphore_wait(barrier, nc // 2)
+
+    far = []
+    for p in range(pieces):
+        here = pl.ds(p * size, size)
+        for j in range(1, nc // 2):
+            copy = remote(
+                block_ref.at[here], out_ref.at[here, columns(my_col)],
+                send.at[j, p], recv.at[j, p], across(j),
+            )
+            copy.start()
+            far.append((p, j, copy))
+    beside = remote(block_ref, out_ref.at[:, columns(my_col)], near.at[0], near.at[1], partner)
+    beside.start()
+    own = pltpu.make_async_copy(block_ref, out_ref.at[:, columns(my_col)], near.at[2])
+    own.start()
+    hops = []
+    for p, j, copy in far:
+        copy.wait_recv()
+        source = lax.rem(my_col - 2 * j + nc, nc)
+        spot = out_ref.at[pl.ds(p * size, size), columns(source)]
+        hop = remote(spot, spot, pass_on.at[j, p], get.at[j, p], partner)
+        hop.start()
+        hops.append(hop)
+    own.wait()
+    beside.wait()
+    for hop in hops:
+        hop.wait()
+    for _, _, copy in far:
+        copy.wait_send()
+
+
+def gather_panel(block, nc):
+    rows, wide = block.shape
+    pieces = 8
+    if nc % 2 or wide % LANES or rows % (SUB * pieces):
+        return lax.all_gather(block, "col", axis=1, tiled=True)
+    dma = pltpu.SemaphoreType.DMA
+    return pl.pallas_call(
+        functools.partial(gather_kernel, nc, pieces),
+        out_shape=jax.ShapeDtypeStruct((rows, wide * nc), jnp.float32),
+        in_specs=[pl.BlockSpec(memory_space=pltpu.VMEM)],
+        out_specs=pl.BlockSpec(memory_space=pl.ANY),
+        scratch_shapes=[dma((nc // 2, pieces))] * 4 + [dma((3,))],
+        compiler_params=pltpu.CompilerParams(collective_id=1, has_side_effects=True),
+        name="gather_panel",
+    )(block)
+
+
 def on_device(nr, nc, panel_block, trailing):
-    gathered = lax.all_gather(panel_block, "col", axis=1, tiled=True)
+    gathered = gather_panel(panel_block, nc)
     share = inner_products(gathered, trailing)
     projected = lax.psum(share, "row")
     gathered, share = lax.optimization_barrier((gathered, share))

time: 186 us -> 176 us (0.946)
  waiting for transfers between devices: 62.1 us -> 9.87 us
  Pallas kernels: 79.9 us -> 122 us
    all_gather x1 -> x0, waiting for transfers between devices: 51.5 us -> none  [on_device(): gathered = lax.all_gather(panel_block, 'col', axis=1, tiled=True)]
    pallas_call x0 -> x1, Pallas kernels: none -> 41.6 us  [gather_panel(): pl.pallas_call(functools.partial(gather_kernel, nc, pieces), out_shape=ja...]
  transfers between devices with their start and end apart: 2 -> 1, of which waited for: 2 -> 1; matrix products, arithmetic and copies ran while one was open for 5% -> 5% of each run, Pallas kernels for 37% -> 39%
where the time goes in v3:
time: 176 us
  Pallas kernels  122 us (69%)
  matrix products  29.6 us (17%)
  between operations  14.1 us (8%)
  waiting for transfers between devices  9.87 us (6%)
    pallas_call x1, Pallas kernels, gather_panel(): pl.pallas_call(functools.partial(gather_kernel, nc, pieces), out_shape=ja...  41.6 us
    pallas_call x1, Pallas kernels, sum_gram(): pl.pallas_call(functools.partial(gram_kernel, nr, nc), out_shape=jax.Shap...  35.3 us
    pallas_call x1, Pallas kernels, factor(): pl.pallas_call(factor_kernel, out_shape=(shape, shape), in_specs=[spec],...  33.4 us
    dot_general x3, matrix products, inner_products(): lax.dot_general(left, right, (((0,), (0,)), ((), ())), precision=precisio...  27 us
    pallas_call x1, Pallas kernels, update(): pl.pallas_call(update_kernel, grid=(rows // tile,), out_shape=jax.ShapeDt...  12 us
    psum x1, waiting for transfers between devices, on_device(): projected = lax.psum(share, 'row')  9.86 us
  transfers between devices with their start and end apart: 1, of which 1 were waited for; matrix products, arithmetic and copies ran while one was open for 5% of the time, Pallas kernels for 39%

profile of v3, /device:TPU:0, one launch (start us, length us, event | category | flops | bytes accessed | tf_op | source)
XLA Modules:
  0.0 175.9 jit_solution(14311932407396270181)
XLA Ops:
  7.2 0.0 all-reduce.2.cloned.1.call-start
  7.2 41.6 %gather_panel.1.panel_ref = f32[3072,512]{1,0:T(8,128)} custom-call(f32[3072,128]{1,0:T(8,128)} %block_ref.1), custom_call_target="tpu_custom_call" | custom-call | tf_op jit(solution)/shard_map/gather_panel/pallas_call | solution.py:347
  48.8 0.0 copy-start
  48.8 14.9 %fusion = f32[512,512]{1,0:T(8,128)} fusion(f32[3072,512]{1,0:T(8,128)} %gather_panel.1.panel_ref, f32[3072,512]{1,0:T(8,128)} %trailing_ref.1), kind=kOutput, calls=%fused_computation | convolution fusion | flops 4831838208 | bytes 13631488 | tf_op jit(solution)/shard_map/dot_general | solution.py:17
  63.7 0.0 all-reduce.2.cloned.1.call-update
  63.8 0.0 copy-done
  63.8 8.5 %fusion.1.part_ref = f32[512,128]{1,0:T(8,128)} fusion(f32[3072,512]{1,0:T(8,128)} %gather_panel.1.panel_ref, f32[3072,128]{1,0:T(8,128)S(1)} %copy-done), kind=kOutput, calls=%fused_computation.1 | convolution fusion | flops 1207959552 | bytes 8126464 | tf_op jit(solution)/shard_map/dot_general | solution.py:17
  72.3 35.3 %sum_gram.1.gram_ref = f32[512,512]{1,0:T(8,128)} custom-call(f32[512,128]{1,0:T(8,128)} %fusion.1.part_ref), custom_call_target="tpu_custom_call" | custom-call | flops 100000 | bytes 20000000 | tf_op jit(solution)/shard_map/sum_gram/pallas_call | solution.py:218
  107.6 33.4 %factor.1 = (f32[512,512]{1,0:T(8,128)}, f32[512,512]{1,0:T(8,128)}) custom-call(f32[512,512]{1,0:T(8,128)} %sum_gram.1.gram_ref), custom_call_target="tpu_custom_call" | custom-call | flops 536870912 | bytes 3145728 | tf_op jit(solution)/shard_map/factor/pallas_call | solution.py:117
  141.0 9.9 %all-reduce.2.cloned.1.call-done = f32[512,512]{1,0:T(8,128)} async-done(((f32[512,512]{1,0:T(8,128)}), f32[512,512]{1,0:T(8,128)}) %all-reduce.2.cloned.1.call-update) | async-done | bytes 1048592 | tf_op jit(solution)/shard_map/psum | solution.py:361
  150.9 2.5 %fusion.2 = f32[512,512]{1,0:T(8,128)S(1)} fusion(f32[512,512]{1,0:T(8,128)} %get-tuple-element.8, f32[512,512]{1,0:T(8,128)} %all-reduce.2.cloned.1.call-done), kind=kOutput, calls=%fused_computation.2 | convolution fusion | flops 805306368 | bytes 3145728 | tf_op jit(solution)/shard_map/dot_general | solution.py:23
  153.4 0.0 copy-start.1
  153.4 3.6 %fusion.3.weights_ref = f32[512,512]{1,0:T(8,128)} fusion(f32[512,512]{1,0:T(8,128)} %get-tuple-element.8, f32[512,512]{1,0:T(8,128)S(1)} %fusion.2), kind=kOutput, calls=%fused_computation.3 | convolution fusion | flops 805306368 | bytes 3145728 | tf_op jit(solution)/shard_map/dot_general | solution.py:17
  157.1 12.0 %update.1 = f32[3072,512]{1,0:T(8,128)} custom-call(f32[3072,512]{1,0:T(8,128)} %gather_panel.1.panel_ref, f32[512,512]{1,0:T(8,128)} %fusion.3.weights_ref, f32[3072,512]{1,0:T(8,128)} %trailing_ref.1), custom_call_target="tpu_custom_call" | custom-call | flops 4831838208 | bytes 18874368 | tf_op jit(solution)/shard_map/update/pallas_call | solution.py:264
  169.1 0.0 copy-done.1
Async XLA Ops:
  7.2 143.7 %all-reduce.2.cloned.1.call-start = ((), (), s32[]{:S(2)}) async-start(), calls=%async_computation | async-start | bytes 2097152 | tf_op jit(solution)/shard_map/psum | solution.py:361
  48.8 14.9 %copy-start = (f32[3072,128]{1,0:T(8,128)S(1)}, f32[3072,128]{1,0:T(8,128)}, u32[]{:S(2)}) copy-start(f32[3072,128]{1,0:T(8,128)} %block_ref.1) | copy-start | bytes 4718596
  153.4 15.7 %copy-start.1 = (f32[512,512]{1,0:T(8,128)}, f32[512,512]{1,0:T(8,128)S(1)}, u32[]{:S(2)}) copy-start(f32[512,512]{1,0:T(8,128)S(1)} %fusion.2) | copy-start | bytes 3145732
Sparse Core Ops, SparseCore 0:
  63.9 86.9 all-reduce.1
